TPU v7x, 256 devices: a whole 4x4x8 slice. The times are simulated.
256 devices in a mesh: sub: 32 (over z, x), agg: 8 (over y, core).
Axes of the slice: x: 4, y: 4, z: 8, core: 2. Of those that a mesh axis runs over, the one named last changes fastest.
Arguments:
- dual_load: float32 [8, 32, 64, 1536], P('agg', 'sub'), may hold values from -58 to 58
- interface_inverse: bfloat16 [8, 32, 1536, 1536], P('agg', 'sub'), may hold values from -1 to 2.5, as said below
- dirichlet: bfloat16 [8, 32, 1536, 1536], P('agg', 'sub'), may hold values from -1 to 2.5, as said below
- coupling: bfloat16 [8, 32, 128, 1536], P('agg', 'sub'), may hold values from -0.15625 to 0.15625
- neighbours: int32 [8, 32, 8], P('agg', 'sub'), may hold values from -1 to 31, as said below
- face_counts: int32 [8, 32, 8], P('agg', 'sub'), may hold values from 0 to 192, as said below
- owners: int32 [8, 32, 128, 1], P('agg', 'sub'), may hold values from 0 to 7; in each aligned block of 128 rows (0 to 127, 128 to 255, ..., all dimensions but the last counted through in order) at most 48 rows name the same one
- primal_rows: int32 [8, 32, 128], P('agg', 'sub'), may hold values from 0 to 1023
- coarse_inverse: float32 [8, 1024, 1024], P('agg', 'sub'), may hold values from -1 to 1.5, as said below
Outputs:
- solution: float32 [8, 32, 64, 1536], P('agg', 'sub')
- residual: float32 [8, 32, 64, 1536], P('agg', 'sub')
Inputs may be any that keep to these rules, and one draw needn't show every extreme that they name: `neighbours`: each subdomain lists peers of its own aggregate by their index along sub, -1 in empty slots; no peer twice; if j lists i then i lists j; every listed peer lies within a cyclic distance of 4 along sub. `face_counts`: 0 exactly in empty slots, 48 or more elsewhere; both sides of a face give the same count and hold its rows in the same order. `owners`: among the 128 primal rows of one subdomain no aggregate is named more than 48 times. `interface_inverse`: each subdomain's matrix is symmetric positive definite. `dirichlet`: each subdomain's matrix is symmetric positive definite. `coarse_inverse`: each aggregate's matrix is symmetric positive definite.
All inputs are finite; a program needn't handle non-finite values.
Results may differ from a plain program's by a relative error of at most 0.011.
Values sent between devices are 32-bit elements; how exact they have to be, the bound alone decides.
No kernel may reach another device: no remote copies, remote signals or barrier semaphores. Data moves between devices by JAX's collectives and lax.ppermute only.
A program may use at most 128 MiB of HBM per device.

v0:
```python
import jax
import jax.numpy as jnp
from jax import lax
from jax.sharding import PartitionSpec as P

NC = 1024
CAP = 48
ITERS = 2
FULL_PRECISION = lax.Precision.HIGHEST
CONTRACT_LAST = (((1,), (1,)), ((), ()))


def from_behind_2(block, axis, distance):
    devices = range(lax.axis_size(axis))
    route = [((i - distance) % len(devices), i) for i in devices]
    return lax.ppermute(block, axis, route)


def shards(
    dual_load,
    interface_inverse,
    dirichlet,
    coupling,
    neighbours,
    face_counts,
    owners,
    primal_rows,
    coarse_inverse,
):
    inverse_block = interface_inverse[0, 0]
    dirichlet_block = dirichlet[0, 0]
    coupling_block = coupling[0, 0]
    peer_list = neighbours[0, 0]
    count_list = face_counts[0, 0]
    sub_count = lax.axis_size("sub")
    agg_count = lax.axis_size("agg")
    position = lax.axis_index("sub")
    slot_count = peer_list.shape[0]
    inner_order = inverse_block.shape[0]
    face_depth = inner_order // slot_count
    reach = min(4, (sub_count - 1) // 2)
    inside = (
        (jnp.arange(face_depth, dtype=jnp.int32)[None, :] < count_list[:, None])
        .reshape(1, inner_order)
        .astype(jnp.float32)
    )

    def assemble(local):
        case_count = local.shape[0]
        faces = local.reshape(case_count, slot_count, face_depth)
        placed = jnp.zeros_like(faces)
        for distance in range(1, reach + 1):
            ahead = (position + distance) % sub_count
            behind = (position + sub_count - distance) % sub_count
            to_ahead = (peer_list == ahead).astype(jnp.float32)[None, :, None]
            to_behind = (peer_list == behind).astype(jnp.float32)[None, :, None]
            upward = jnp.sum(faces * to_ahead, axis=1)
            downward = jnp.sum(faces * to_behind, axis=1)
            from_behind = from_behind_2(upward, "sub", distance)
            from_ahead = from_behind_2(downward, "sub", -distance)
            placed = (
                placed + to_behind * from_behind[:, None, :] + to_ahead * from_ahead[:, None, :]
            )
        return inside * (local + placed.reshape(case_count, inner_order))

    owner_ids = owners[0, 0, :, 0]
    row_ids = primal_rows[0, 0]
    owner_hot = (owner_ids[:, None] == jnp.arange(agg_count, dtype=jnp.int32)[None, :]).astype(
        jnp.int32
    )
    earlier = jnp.cumsum(owner_hot, axis=0) - owner_hot
    owner_rank = jnp.sum(earlier * owner_hot, axis=1)
    slot_index = owner_ids * CAP + owner_rank
    packing = slot_index[:, None] == jnp.arange(agg_count * CAP, dtype=jnp.int32)[None, :]
    packing_float = packing.astype(jnp.float32)
    sent_rows = jnp.sum(packing.astype(jnp.int32) * (row_ids[:, None] + 1), axis=0) - 1
    got_rows = lax.all_to_all(sent_rows, "agg", split_axis=0, concat_axis=0, tiled=True)
    scatter_hot = (got_rows[:, None] == jnp.arange(NC, dtype=jnp.int32)[None, :]).astype(
        jnp.float32
    )
    inverse_rows = coarse_inverse[0]

    def precondition(field):
        packed = field.astype(jnp.bfloat16)
        return assemble(
            inside * jnp.dot(packed, dirichlet_block, preferred_element_type=jnp.float32)
        )

    def residual_norm(first, second):
        return lax.psum(jnp.sum(first * second, axis=1), ("sub", "agg"))

    rhs = assemble(inside * dual_load[0, 0])
    solution = jnp.zeros_like(rhs)
    residual = rhs
    precond = precondition(residual)
    direction = precond
    residual_dot = residual_norm(residual, precond)
    for iteration in range(ITERS):
        operator_packed = direction.astype(jnp.bfloat16)
        own = jnp.dot(operator_packed, inverse_block, preferred_element_type=jnp.float32)
        terms = lax.dot_general(
            operator_packed, coupling_block, CONTRACT_LAST, preferred_element_type=jnp.float32
        )
        outgoing = jnp.dot(terms, packing_float, precision=FULL_PRECISION)
        gathered = jnp.dot(
            lax.all_to_all(outgoing, "agg", split_axis=1, concat_axis=1, tiled=True),
            scatter_hot,
            precision=FULL_PRECISION,
        )
        coarse_rhs = lax.psum(gathered, "sub")
        partial_rows = lax.dot_general(
            coarse_rhs, inverse_rows, CONTRACT_LAST, precision=FULL_PRECISION
        )
        coarse_sol = lax.all_gather(partial_rows, "sub", axis=1, tiled=True)
        answer = lax.dot_general(coarse_sol, scatter_hot, CONTRACT_LAST, precision=FULL_PRECISION)
        returned = lax.all_to_all(answer, "agg", split_axis=1, concat_axis=1, tiled=True)
        local_back = lax.dot_general(
            returned, packing_float, CONTRACT_LAST, precision=FULL_PRECISION
        )
        correction = jnp.dot(
            local_back.astype(jnp.bfloat16), coupling_block, preferred_element_type=jnp.float32
        )
        image = assemble(inside * (own + correction))
        alpha = (residual_dot / lax.psum(jnp.sum(direction * image, axis=1), ("sub", "agg")))[
            :, None
        ]
        solution = solution + alpha * direction
        residual = residual - alpha * image
        if iteration + 1 < ITERS:
            precond = precondition(residual)
            next_dot = residual_norm(residual, precond)
            direction = precond + (next_dot / residual_dot)[:, None] * direction
            residual_dot = next_dot
    return (solution[None, None], residual[None, None])


def solution(mesh):
    in_specs = (
        P("agg", "sub", None, None),
        P("agg", "sub", None, None),
        P("agg", "sub", None, None),
        P("agg", "sub", None, None),
        P("agg", "sub", None),
        P("agg", "sub", None),
        P("agg", "sub", None, None),
        P("agg", "sub", None),
        P("agg", "sub", None),
    )
    out_specs = (P("agg", "sub", None, None), P("agg", "sub", None, None))
    return jax.shard_map(shards, mesh=mesh, in_specs=in_specs, out_specs=out_specs, check_vma=False)
```

profile of v0, /device:TPU:1, one launch (start us, length us, event | category | flops | bytes accessed | tf_op | source)
XLA Modules:
  0.0 917.8 jit_solution(6425770265424465426)
XLA Ops:
  13.6 6.6 collective-permute-start.1
  20.4 2.7 collective-permute-start.7
  28.4 2.6 collective-permute-start.3
  50.8 5.2 fusion.8
  58.0 2.5 multiply_reduce_fusion.31
  60.5 4.7 collective-permute-start.11
  65.2 2.7 collective-permute-start.9
  76.5 10.1 %all-to-all-start.1 = ((s32[8,48,1]{1,2,0:T(1,128)}), s32[8,48,1]{1,2,0:T(1,128)}, u32[]{:S(2)}, u32[]{:S(2)}) async-start(s32[8,48,1]{1,2,0:T(1,128)} %bitcast.111), calls=%async_computation.1 | async-start | bytes 8192 | tf_op jit(solution)/shard_map/all_to_all | solution.py:77
  119.4 4.8 all-to-all-start
  136.4 138.3 %all-reduce.4.cloned.1.call-done = f32[64,1024]{1,0:T(8,128)} async-done(((f32[64,1024]{1,0:T(8,128)}), f32[64,1024]{1,0:T(8,128)}) %all-reduce.4.cloned.1.call-update) | async-done | bytes 262160 | tf_op jit(solution)/shard_map/psum | solution.py:110
  275.9 35.9 %all_gather.6 = f32[64,1024]{0,1:T(8,128)S(1)} all-gather(f32[64,32]{0,1:T(8,128)S(1)} %fusion.58), channel_id=1, replica_groups=mesh['sub'=32,'agg'=8] {'sub'}, dimensions={1}, use_global_device_ids=true | all-gather | bytes 270336 | tf_op jit(solution)/shard_map/all_gather | solution.py:114
  315.8 26.7 %all_to_all.54 = f32[8,1,3072]{2,1,0:T(1,128)} all-to-all(f32[8,1,3072]{2,1,0:T(1,128)} %reshape.670), channel_id=1, replica_groups=mesh['sub'=32,'agg'=8] {'agg'}, dimensions={0} | all-to-all | bytes 196608 | tf_op jit(solution)/shard_map/all_to_all | solution.py:116
  348.1 4.0 fusion.23
  354.1 3.2 multiply_reduce_fusion.23
  360.2 4.5 collective-permute-start.17
  364.7 3.8 collective-permute-start.21
  368.5 2.7 collective-permute-start.23
  394.4 3.9 multiply_reduce_fusion.42
  398.5 77.6 %all-reduce = (f32[64]{0:T(128)S(1)}, f32[64]{0:T(128)S(1)}) all-reduce(f32[64]{0:T(128)S(1)} %get-tuple-element.43, f32[64]{0:T(128)S(1)} %get-tuple-element.42), channel_id=1, replica_groups=mesh['sub'=32,'agg'=8] {'sub','agg'}, use_global_device_ids=true, to_apply=%region_17.18 | all-reduce | flops 128 | bytes 1024 | tf_op jit(solution)/shard_map/psum | solution.py:90
  477.2 3.3 fusion.11
  488.2 3.5 collective-permute-start.29
  491.7 2.7 collective-permute-start.31
  505.9 77.6 %psum.45 = f32[64]{0:T(128)S(1)} all-reduce(f32[64]{0:T(128)S(1)} %get-tuple-element.48), channel_id=1, replica_groups=mesh['sub'=32,'agg'=8] {'sub','agg'}, use_global_device_ids=true, to_apply=%region_41.42 | all-reduce | flops 64 | bytes 512 | tf_op jit(solution)/shard_map/psum | solution.py:90
  585.7 8.1 all_to_all.55
  596.3 136.3 %all-reduce.6.cloned.1.call-done = f32[64,1024]{1,0:T(8,128)} async-done(((f32[64,1024]{1,0:T(8,128)}), f32[64,1024]{1,0:T(8,128)}) %all-reduce.6.cloned.1.call-update) | async-done | bytes 262160 | tf_op jit(solution)/shard_map/psum | solution.py:110
  733.9 35.9 %all_gather.7 = f32[64,1024]{0,1:T(8,128)S(1)} all-gather(f32[64,32]{0,1:T(8,128)S(1)} %fusion.56), channel_id=1, replica_groups=mesh['sub'=32,'agg'=8] {'sub'}, dimensions={1}, use_global_device_ids=true | all-gather | bytes 270336 | tf_op jit(solution)/shard_map/all_gather | solution.py:114
  770.8 26.7 %all_to_all.56 = f32[8,1,3072]{2,1,0:T(1,128)S(1)} all-to-all(f32[8,1,3072]{2,1,0:T(1,128)S(1)} %reshape.674), channel_id=1, replica_groups=mesh['sub'=32,'agg'=8] {'agg'}, dimensions={0} | all-to-all | bytes 196608 | tf_op jit(solution)/shard_map/all_to_all | solution.py:116
  799.1 3.3 fusion.20
  807.2 4.5 collective-permute-start.33
  811.7 3.6 collective-permute-start.37
  815.3 2.7 collective-permute-start.39
  831.3 77.7 %psum.47 = f32[64]{0:T(128)S(1)} all-reduce(f32[64]{0:T(128)S(1)} %get-tuple-element.46), channel_id=1, replica_groups=mesh['sub'=32,'agg'=8] {'sub','agg'}, use_global_device_ids=true, to_apply=%region_52.53 | all-reduce | flops 64 | bytes 512 | tf_op jit(solution)/shard_map/psum | solution.py:124
  (347 shorter events, 174.0 us)
Async XLA Ops:
  11.5 35.6 %collective-permute-start = (f32[64,192]{1,0:T(8,128)S(1)}, f32[64,192]{1,0:T(8,128)}, u32[]{:S(2)}, u32[]{:S(2)}) collective-permute-start(f32[64,192]{1,0:T(8,128)S(1)} %get-tuple-element.2), channel_id=1, source_target_pairs={{248,0},{0,8},{8,16},{16,24},{24,32},{32,40},{40,48},{48,56},{56,6... | collective-permute-start | bytes 147464 | tf_op jit(solution)/shard_map/ppermute | solution.py:16
  13.6 29.9 %collective-permute-start.1 = (f32[64,192]{1,0:T(8,128)}, f32[64,192]{1,0:T(8,128)}, u32[]{:S(2)}, u32[]{:S(2)}) collective-permute-start(f32[64,192]{1,0:T(8,128)} %get-tuple-element.3), channel_id=1, source_target_pairs={{8,0},{16,8},{24,16},{32,24},{40,32},{48,40},{56,48},{64,56},{72,6... | collective-permute-start | bytes 147464 | tf_op jit(solution)/shard_map/ppermute | solution.py:16
  20.4 10.7 %collective-permute-start.7 = (f32[64,192]{1,0:T(8,128)S(1)}, f32[64,192]{1,0:T(8,128)S(1)}, u32[]{:S(2)}, u32[]{:S(2)}) collective-permute-start(f32[64,192]{1,0:T(8,128)S(1)} %get-tuple-element.9), channel_id=1, source_target_pairs={{32,0},{40,8},{48,16},{56,24},{64,32},{72,40},{80,48},{88,56},{96,... | collective-permute-start | bytes 147464 | tf_op jit(solution)/shard_map/ppermute | solution.py:16
  26.0 13.9 %collective-permute-start.2 = (f32[64,192]{1,0:T(8,128)}, f32[64,192]{1,0:T(8,128)}, u32[]{:S(2)}, u32[]{:S(2)}) collective-permute-start(f32[64,192]{1,0:T(8,128)} %get-tuple-element.4), channel_id=1, source_target_pairs={{240,0},{248,8},{0,16},{8,24},{16,32},{24,40},{32,48},{40,56},{48,... | collective-permute-start | bytes 147464 | tf_op jit(solution)/shard_map/ppermute | solution.py:16
  28.4 9.6 %collective-permute-start.3 = (f32[64,192]{1,0:T(8,128)S(1)}, f32[64,192]{1,0:T(8,128)}, u32[]{:S(2)}, u32[]{:S(2)}) collective-permute-start(f32[64,192]{1,0:T(8,128)S(1)} %get-tuple-element.5), channel_id=1, source_target_pairs={{16,0},{24,8},{32,16},{40,24},{48,32},{56,40},{64,48},{72,56},{80,... | collective-permute-start | bytes 147464 | tf_op jit(solution)/shard_map/ppermute | solution.py:16
  68.6 41.9 %collective-permute-start.8 = (f32[64,192]{1,0:T(8,128)S(1)}, f32[64,192]{1,0:T(8,128)S(1)}, u32[]{:S(2)}, u32[]{:S(2)}) collective-permute-start(f32[64,192]{1,0:T(8,128)S(1)} %get-tuple-element.34), channel_id=1, source_target_pairs={{248,0},{0,8},{8,16},{16,24},{24,32},{32,40},{40,48},{48,56},{56,6... | collective-permute-start | bytes 147464 | tf_op jit(solution)/shard_map/ppermute | solution.py:16
  68.7 39.0 %collective-permute-start.15 = (f32[64,192]{1,0:T(8,128)S(1)}, f32[64,192]{1,0:T(8,128)S(1)}, u32[]{:S(2)}, u32[]{:S(2)}) collective-permute-start(f32[64,192]{1,0:T(8,128)S(1)} %get-tuple-element.35), channel_id=1, source_target_pairs={{32,0},{40,8},{48,16},{56,24},{64,32},{72,40},{80,48},{88,56},{96,... | collective-permute-start | bytes 147464 | tf_op jit(solution)/shard_map/ppermute | solution.py:16
  68.8 35.2 %collective-permute-start.14 = (f32[64,192]{1,0:T(8,128)S(1)}, f32[64,192]{1,0:T(8,128)}, u32[]{:S(2)}, u32[]{:S(2)}) collective-permute-start(f32[64,192]{1,0:T(8,128)S(1)} %get-tuple-element.36), channel_id=1, source_target_pairs={{224,0},{232,8},{240,16},{248,24},{0,32},{8,40},{16,48},{24,56},{3... | collective-permute-start | bytes 147464 | tf_op jit(solution)/shard_map/ppermute | solution.py:16
  71.9 28.5 %collective-permute-start.13 = (f32[64,192]{1,0:T(8,128)S(1)}, f32[64,192]{1,0:T(8,128)}, u32[]{:S(2)}, u32[]{:S(2)}) collective-permute-start(f32[64,192]{1,0:T(8,128)S(1)} %get-tuple-element.37), channel_id=1, source_target_pairs={{24,0},{32,8},{40,16},{48,24},{56,32},{64,40},{72,48},{80,56},{88,... | collective-permute-start | bytes 147464 | tf_op jit(solution)/shard_map/ppermute | solution.py:16
  73.5 23.3 %collective-permute-start.12 = (f32[64,192]{1,0:T(8,128)S(1)}, f32[64,192]{1,0:T(8,128)}, u32[]{:S(2)}, u32[]{:S(2)}) collective-permute-start(f32[64,192]{1,0:T(8,128)S(1)} %get-tuple-element.38), channel_id=1, source_target_pairs={{232,0},{240,8},{248,16},{0,24},{8,32},{16,40},{24,48},{32,56},{40... | collective-permute-start | bytes 147464 | tf_op jit(solution)/shard_map/ppermute | solution.py:16
  76.5 42.9 %all-to-all-start.1 = ((s32[8,48,1]{1,2,0:T(1,128)}), s32[8,48,1]{1,2,0:T(1,128)}, u32[]{:S(2)}, u32[]{:S(2)}) async-start(s32[8,48,1]{1,2,0:T(1,128)} %bitcast.111), calls=%async_computation.1 | async-start | bytes 8192 | tf_op jit(solution)/shard_map/all_to_all | solution.py:77
  119.4 9.9 %all-to-all-start = ((f32[8,1,3072]{2,1,0:T(1,128)}), f32[8,1,3072]{2,1,0:T(1,128)}, u32[]{:S(2)}, u32[]{:S(2)}) async-start(f32[8,1,3072]{2,1,0:T(1,128)} %reshape.668), calls=%async_computation | async-start | bytes 196608 | tf_op jit(solution)/shard_map/all_to_all | solution.py:106
  124.2 150.4 %all-reduce.4.cloned.1.call-start = ((), (), s32[]{:S(2)}) async-start(), calls=%async_computation.5 | async-start | bytes 524288 | tf_op jit(solution)/shard_map/psum | solution.py:110
  136.3 596.3 %all-reduce.6.cloned.1.call-start = ((), (), s32[]{:S(2)}) async-start(), calls=%async_computation.6 | async-start | bytes 524288 | tf_op jit(solution)/shard_map/psum | solution.py:110
  357.3 11.3 %collective-permute-start.19 = (f32[64,192]{1,0:T(8,128)S(1)}, f32[64,192]{1,0:T(8,128)}, u32[]{:S(2)}, u32[]{:S(2)}) collective-permute-start(f32[64,192]{1,0:T(8,128)S(1)} %get-tuple-element.31), channel_id=1, source_target_pairs={{16,0},{24,8},{32,16},{40,24},{48,32},{56,40},{64,48},{72,56},{80,... | collective-permute-start | bytes 147464 | tf_op jit(solution)/shard_map/ppermute | solution.py:16
  359.2 9.3 %collective-permute-start.18 = (f32[64,192]{1,0:T(8,128)S(1)}, f32[64,192]{1,0:T(8,128)}, u32[]{:S(2)}, u32[]{:S(2)}) collective-permute-start(f32[64,192]{1,0:T(8,128)S(1)} %get-tuple-element.32), channel_id=1, source_target_pairs={{240,0},{248,8},{0,16},{8,24},{16,32},{24,40},{32,48},{40,56},{48,... | collective-permute-start | bytes 147464 | tf_op jit(solution)/shard_map/ppermute | solution.py:16
  360.2 11.0 %collective-permute-start.17 = (f32[64,192]{1,0:T(8,128)S(1)}, f32[64,192]{1,0:T(8,128)}, u32[]{:S(2)}, u32[]{:S(2)}) collective-permute-start(f32[64,192]{1,0:T(8,128)S(1)} %get-tuple-element.33), channel_id=1, source_target_pairs={{8,0},{16,8},{24,16},{32,24},{40,32},{48,40},{56,48},{64,56},{72,6... | collective-permute-start | bytes 147464 | tf_op jit(solution)/shard_map/ppermute | solution.py:16
  364.7 20.5 %collective-permute-start.20 = (f32[64,192]{1,0:T(8,128)}, f32[64,192]{1,0:T(8,128)}, u32[]{:S(2)}, u32[]{:S(2)}) collective-permute-start(f32[64,192]{1,0:T(8,128)} %get-tuple-element.30), channel_id=1, source_target_pairs={{232,0},{240,8},{248,16},{0,24},{8,32},{16,40},{24,48},{32,56},{40... | collective-permute-start | bytes 147464 | tf_op jit(solution)/shard_map/ppermute | solution.py:16
  364.7 22.3 %collective-permute-start.21 = (f32[64,192]{1,0:T(8,128)}, f32[64,192]{1,0:T(8,128)}, u32[]{:S(2)}, u32[]{:S(2)}) collective-permute-start(f32[64,192]{1,0:T(8,128)} %get-tuple-element.29), channel_id=1, source_target_pairs={{24,0},{32,8},{40,16},{48,24},{56,32},{64,40},{72,48},{80,56},{88,... | collective-permute-start | bytes 147464 | tf_op jit(solution)/shard_map/ppermute | solution.py:16
  368.5 20.4 %collective-permute-start.22 = (f32[64,192]{1,0:T(8,128)}, f32[64,192]{1,0:T(8,128)}, u32[]{:S(2)}, u32[]{:S(2)}) collective-permute-start(f32[64,192]{1,0:T(8,128)} %get-tuple-element.28), channel_id=1, source_target_pairs={{224,0},{232,8},{240,16},{248,24},{0,32},{8,40},{16,48},{24,56},{3... | collective-permute-start | bytes 147464 | tf_op jit(solution)/shard_map/ppermute | solution.py:16
  368.5 22.2 %collective-permute-start.23 = (f32[64,192]{1,0:T(8,128)}, f32[64,192]{1,0:T(8,128)}, u32[]{:S(2)}, u32[]{:S(2)}) collective-permute-start(f32[64,192]{1,0:T(8,128)} %get-tuple-element.27), channel_id=1, source_target_pairs={{32,0},{40,8},{48,16},{56,24},{64,32},{72,40},{80,48},{88,56},{96,... | collective-permute-start | bytes 147464 | tf_op jit(solution)/shard_map/ppermute | solution.py:16
  371.2 21.3 %collective-permute-start.16 = (f32[64,192]{1,0:T(8,128)}, f32[64,192]{1,0:T(8,128)}, u32[]{:S(2)}, u32[]{:S(2)}) collective-permute-start(f32[64,192]{1,0:T(8,128)} %get-tuple-element.26), channel_id=1, source_target_pairs={{248,0},{0,8},{8,16},{16,24},{24,32},{32,40},{40,48},{48,56},{56,6... | collective-permute-start | bytes 147464 | tf_op jit(solution)/shard_map/ppermute | solution.py:16
  482.7 9.0 collective-permute-start.27
  485.6 8.7 collective-permute-start.25
  488.2 8.7 collective-permute-start.29
  491.7 8.8 collective-permute-start.31
  804.3 11.0 %collective-permute-start.35 = (f32[64,192]{1,0:T(8,128)S(1)}, f32[64,192]{1,0:T(8,128)S(1)}, u32[]{:S(2)}, u32[]{:S(2)}) collective-permute-start(f32[64,192]{1,0:T(8,128)S(1)} %get-tuple-element.15), channel_id=1, source_target_pairs={{16,0},{24,8},{32,16},{40,24},{48,32},{56,40},{64,48},{72,56},{80,... | collective-permute-start | bytes 147464 | tf_op jit(solution)/shard_map/ppermute | solution.py:16
  806.2 9.1 collective-permute-start.34
  807.2 10.8 %collective-permute-start.33 = (f32[64,192]{1,0:T(8,128)S(1)}, f32[64,192]{1,0:T(8,128)S(1)}, u32[]{:S(2)}, u32[]{:S(2)}) collective-permute-start(f32[64,192]{1,0:T(8,128)S(1)} %get-tuple-element.17), channel_id=1, source_target_pairs={{8,0},{16,8},{24,16},{32,24},{40,32},{48,40},{56,48},{64,56},{72,6... | collective-permute-start | bytes 147464 | tf_op jit(solution)/shard_map/ppermute | solution.py:16
  811.7 10.3 %collective-permute-start.37 = (f32[64,192]{1,0:T(8,128)}, f32[64,192]{1,0:T(8,128)}, u32[]{:S(2)}, u32[]{:S(2)}) collective-permute-start(f32[64,192]{1,0:T(8,128)} %get-tuple-element.13), channel_id=1, source_target_pairs={{24,0},{32,8},{40,16},{48,24},{56,32},{64,40},{72,48},{80,56},{88,... | collective-permute-start | bytes 147464 | tf_op jit(solution)/shard_map/ppermute | solution.py:16
  815.3 10.3 %collective-permute-start.39 = (f32[64,192]{1,0:T(8,128)S(1)}, f32[64,192]{1,0:T(8,128)}, u32[]{:S(2)}, u32[]{:S(2)}) collective-permute-start(f32[64,192]{1,0:T(8,128)S(1)} %get-tuple-element.11), channel_id=1, source_target_pairs={{32,0},{40,8},{48,16},{56,24},{64,32},{72,40},{80,48},{88,56},{96,... | collective-permute-start | bytes 147464 | tf_op jit(solution)/shard_map/ppermute | solution.py:16
  818.0 9.5 %collective-permute-start.32 = (f32[64,192]{1,0:T(8,128)S(1)}, f32[64,192]{1,0:T(8,128)}, u32[]{:S(2)}, u32[]{:S(2)}) collective-permute-start(f32[64,192]{1,0:T(8,128)S(1)} %get-tuple-element.10), channel_id=1, source_target_pairs={{248,0},{0,8},{8,16},{16,24},{24,32},{32,40},{40,48},{48,56},{56,6... | collective-permute-start | bytes 147464 | tf_op jit(solution)/shard_map/ppermute | solution.py:16
  (68 other events, 2431.6 us)
Sparse Core Ops, SparseCore 0:
  136.4 138.1 all-reduce.3
  596.4 136.1 all-reduce.5
where the time goes:
time: 927 us; the launch traced here: 918 us
  blocking collectives  366 us (39%)
  waiting for transfers between devices  278 us (30%)
  local copies, waits for them, and re-layouts  105 us (11%)
  starting transfers between devices  83.3 us (9%)
  other arithmetic  39.7 us (4%)
  matrix products  30.5 us (3%)
  between operations  15.6 us (2%)
    psum x2, waiting for transfers between devices, shards(): coarse_rhs = lax.psum(gathered, 'sub')  275 us
    psum x2, blocking collectives, residual_norm(): return lax.psum(jnp.sum(first * second, axis=1), ('sub', 'agg'))  155 us
    psum x1, blocking collectives, shards(): lax.psum(jnp.sum(direction * image, axis=1), ('sub', 'agg'))  77.7 us
    all_gather x2, blocking collectives, shards(): coarse_sol = lax.all_gather(partial_rows, 'sub', axis=1, tiled=True)  71.7 us
    ppermute x40, starting transfers between devices, from_behind_2(): return lax.ppermute(block, axis, route)  68.3 us
    all_to_all x2, blocking collectives, shards(): lax.all_to_all(answer, 'agg', split_axis=1, concat_axis=1, tiled=True)  53.4 us
    mul x52, local copies, waits for them, and re-layouts, assemble(): to_behind * from_behind[:, None, :]  46.7 us
    mul x44, local copies, waits for them, and re-layouts, assemble(): to_ahead * from_ahead[:, None, :]  40.9 us
  transfers between devices with their start and end apart: 44, of which 4 were waited for; matrix products, arithmetic and copies ran while one was open for 10% of the time, Pallas kernels for 0%

commit v1 on v0

--- a/solution.py
+++ b/solution.py
@@ -8,6 +8,13 @@
 ITERS = 2
 FULL_PRECISION = lax.Precision.HIGHEST
 CONTRACT_LAST = (((1,), (1,)), ((), ()))
+
+
+def trade_parts(x, name, split, join):
+    size = lax.axis_size(name)
+    shards = jnp.stack(jnp.split(x, size, axis=split), axis=0)
+    shards = lax.all_to_all(shards, name, split_axis=0, concat_axis=0)
+    return jnp.concatenate(shards, axis=join)
 
 
 def from_behind_2(block, axis, distance):
@@ -113,7 +120,7 @@
         )
         coarse_sol = lax.all_gather(partial_rows, "sub", axis=1, tiled=True)
         answer = lax.dot_general(coarse_sol, scatter_hot, CONTRACT_LAST, precision=FULL_PRECISION)
-        returned = lax.all_to_all(answer, "agg", split_axis=1, concat_axis=1, tiled=True)
+        returned = trade_parts(answer, "agg", 1, 1)
         local_back = lax.dot_general(
             returned, packing_float, CONTRACT_LAST, precision=FULL_PRECISION
         )

time: 927 us -> 935 us (level)
  no operation moved by 1% of the time
where the time goes in v1:
time: 935 us; the launch traced here: 926 us
  blocking collectives  366 us (39%)
  waiting for transfers between devices  278 us (30%)
  local copies, waits for them, and re-layouts  113 us (12%)
  starting transfers between devices  83.3 us (9%)
  other arithmetic  39.7 us (4%)
  matrix products  30.3 us (3%)
  between operations  15.6 us (2%)
    psum x2, waiting for transfers between devices, shards(): coarse_rhs = lax.psum(gathered, 'sub')  275 us
    psum x2, blocking collectives, residual_norm(): return lax.psum(jnp.sum(first * second, axis=1), ('sub', 'agg'))  155 us
    psum x1, blocking collectives, shards(): lax.psum(jnp.sum(direction * image, axis=1), ('sub', 'agg'))  77.7 us
    all_gather x2, blocking collectives, shards(): coarse_sol = lax.all_gather(partial_rows, 'sub', axis=1, tiled=True)  71.7 us
    ppermute x40, starting transfers between devices, from_behind_2(): return lax.ppermute(block, axis, route)  68.3 us
    all_to_all x2, blocking collectives, trade_parts(): shards = lax.all_to_all(shards, name, split_axis=0, concat_axis=0)  53.4 us
    mul x52, local copies, waits for them, and re-layouts, assemble(): to_behind * from_behind[:, None, :]  46.7 us
    mul x44, local copies, waits for them, and re-layouts, assemble(): to_ahead * from_ahead[:, None, :]  40.9 us
  transfers between devices with their start and end apart: 44, of which 4 were waited for; matrix products, arithmetic and copies ran while one was open for 10% of the time, Pallas kernels for 0%

profile of v1, /device:TPU:1, one launch (start us, length us, event | category | flops | bytes accessed | tf_op | source)
XLA Modules:
  0.0 925.5 jit_solution(4207860750517160455)
XLA Ops:
  13.6 6.6 collective-permute-start.1
  20.4 2.7 collective-permute-start.7
  28.4 2.6 collective-permute-start.3
  50.8 5.2 fusion.8
  60.5 4.7 collective-permute-start.11
  65.2 2.7 collective-permute-start.9
  76.5 10.1 %all-to-all-start.1 = ((s32[8,48,1]{1,2,0:T(1,128)}), s32[8,48,1]{1,2,0:T(1,128)}, u32[]{:S(2)}, u32[]{:S(2)}) async-start(s32[8,48,1]{1,2,0:T(1,128)} %bitcast.177), calls=%async_computation.1 | async-start | bytes 8192 | tf_op jit(solution)/shard_map/all_to_all | solution.py:84
  119.4 4.8 all-to-all-start
  136.4 138.3 %all-reduce.4.cloned.1.call-done = f32[64,1024]{1,0:T(8,128)} async-done(((f32[64,1024]{1,0:T(8,128)}), f32[64,1024]{1,0:T(8,128)}) %all-reduce.4.cloned.1.call-update) | async-done | bytes 262160 | tf_op jit(solution)/shard_map/psum | solution.py:117
  275.9 35.9 %all_gather.6 = f32[64,1024]{0,1:T(8,128)S(1)} all-gather(f32[64,32]{0,1:T(8,128)S(1)} %fusion.58), channel_id=1, replica_groups=mesh['sub'=32,'agg'=8] {'sub'}, dimensions={1}, use_global_device_ids=true | all-gather | bytes 270336 | tf_op jit(solution)/shard_map/all_gather | solution.py:121
  322.6 26.7 %all_to_all.40 = f32[8,1,3072]{2,1,0:T(1,128)} all-to-all(f32[8,1,3072]{2,1,0:T(1,128)} %reshape.682), channel_id=1, replica_groups=mesh['sub'=32,'agg'=8] {'agg'}, dimensions={0} | all-to-all | bytes 196608 | tf_op jit(solution)/shard_map/all_to_all | solution.py:16
  354.8 4.0 fusion.23
  360.8 3.2 multiply_reduce_fusion.23
  367.0 4.5 collective-permute-start.17
  371.7 3.6 collective-permute-start.21
  375.2 2.7 collective-permute-start.23
  401.1 3.9 multiply_reduce_fusion.42
  405.2 77.6 %all-reduce = (f32[64]{0:T(128)S(1)}, f32[64]{0:T(128)S(1)}) all-reduce(f32[64]{0:T(128)S(1)} %get-tuple-element.43, f32[64]{0:T(128)S(1)} %get-tuple-element.42), channel_id=1, replica_groups=mesh['sub'=32,'agg'=8] {'sub','agg'}, use_global_device_ids=true, to_apply=%region_17.18 | all-reduce | flops 128 | bytes 1024 | tf_op jit(solution)/shard_map/psum | solution.py:97
  483.9 3.3 fusion.11
  492.3 2.6 collective-permute-start.25
  494.9 3.6 collective-permute-start.29
  498.5 2.7 collective-permute-start.31
  512.7 77.6 %psum.45 = f32[64]{0:T(128)S(1)} all-reduce(f32[64]{0:T(128)S(1)} %get-tuple-element.48), channel_id=1, replica_groups=mesh['sub'=32,'agg'=8] {'sub','agg'}, use_global_device_ids=true, to_apply=%region_41.42 | all-reduce | flops 64 | bytes 512 | tf_op jit(solution)/shard_map/psum | solution.py:97
  592.5 8.1 all_to_all.41
  603.1 136.3 %all-reduce.6.cloned.1.call-done = f32[64,1024]{1,0:T(8,128)} async-done(((f32[64,1024]{1,0:T(8,128)}), f32[64,1024]{1,0:T(8,128)}) %all-reduce.6.cloned.1.call-update) | async-done | bytes 262160 | tf_op jit(solution)/shard_map/psum | solution.py:117
  740.6 35.9 %all_gather.7 = f32[64,1024]{0,1:T(8,128)S(1)} all-gather(f32[64,32]{0,1:T(8,128)S(1)} %fusion.56), channel_id=1, replica_groups=mesh['sub'=32,'agg'=8] {'sub'}, dimensions={1}, use_global_device_ids=true | all-gather | bytes 270336 | tf_op jit(solution)/shard_map/all_gather | solution.py:121
  778.5 26.7 %all_to_all.42 = f32[8,1,3072]{2,1,0:T(1,128)S(1)} all-to-all(f32[8,1,3072]{2,1,0:T(1,128)S(1)} %reshape.686), channel_id=1, replica_groups=mesh['sub'=32,'agg'=8] {'agg'}, dimensions={0} | all-to-all | bytes 196608 | tf_op jit(solution)/shard_map/all_to_all | solution.py:16
  806.8 3.3 fusion.20
  814.9 4.5 collective-permute-start.33
  819.4 3.6 collective-permute-start.37
  823.0 2.7 collective-permute-start.39
  839.0 77.7 %psum.47 = f32[64]{0:T(128)S(1)} all-reduce(f32[64]{0:T(128)S(1)} %get-tuple-element.46), channel_id=1, replica_groups=mesh['sub'=32,'agg'=8] {'sub','agg'}, use_global_device_ids=true, to_apply=%region_52.53 | all-reduce | flops 64 | bytes 512 | tf_op jit(solution)/shard_map/psum | solution.py:131
  (365 shorter events, 181.8 us)
Async XLA Ops:
  11.5 35.6 %collective-permute-start = (f32[64,192]{1,0:T(8,128)S(1)}, f32[64,192]{1,0:T(8,128)}, u32[]{:S(2)}, u32[]{:S(2)}) collective-permute-start(f32[64,192]{1,0:T(8,128)S(1)} %get-tuple-element.2), channel_id=1, source_target_pairs={{248,0},{0,8},{8,16},{16,24},{24,32},{32,40},{40,48},{48,56},{56,6... | collective-permute-start | bytes 147464 | tf_op jit(solution)/shard_map/ppermute | solution.py:23
  13.6 29.9 %collective-permute-start.1 = (f32[64,192]{1,0:T(8,128)}, f32[64,192]{1,0:T(8,128)}, u32[]{:S(2)}, u32[]{:S(2)}) collective-permute-start(f32[64,192]{1,0:T(8,128)} %get-tuple-element.3), channel_id=1, source_target_pairs={{8,0},{16,8},{24,16},{32,24},{40,32},{48,40},{56,48},{64,56},{72,6... | collective-permute-start | bytes 147464 | tf_op jit(solution)/shard_map/ppermute | solution.py:23
  20.4 10.7 %collective-permute-start.7 = (f32[64,192]{1,0:T(8,128)S(1)}, f32[64,192]{1,0:T(8,128)S(1)}, u32[]{:S(2)}, u32[]{:S(2)}) collective-permute-start(f32[64,192]{1,0:T(8,128)S(1)} %get-tuple-element.9), channel_id=1, source_target_pairs={{32,0},{40,8},{48,16},{56,24},{64,32},{72,40},{80,48},{88,56},{96,... | collective-permute-start | bytes 147464 | tf_op jit(solution)/shard_map/ppermute | solution.py:23
  26.0 13.9 %collective-permute-start.2 = (f32[64,192]{1,0:T(8,128)}, f32[64,192]{1,0:T(8,128)}, u32[]{:S(2)}, u32[]{:S(2)}) collective-permute-start(f32[64,192]{1,0:T(8,128)} %get-tuple-element.4), channel_id=1, source_target_pairs={{240,0},{248,8},{0,16},{8,24},{16,32},{24,40},{32,48},{40,56},{48,... | collective-permute-start | bytes 147464 | tf_op jit(solution)/shard_map/ppermute | solution.py:23
  28.4 9.6 %collective-permute-start.3 = (f32[64,192]{1,0:T(8,128)S(1)}, f32[64,192]{1,0:T(8,128)}, u32[]{:S(2)}, u32[]{:S(2)}) collective-permute-start(f32[64,192]{1,0:T(8,128)S(1)} %get-tuple-element.5), channel_id=1, source_target_pairs={{16,0},{24,8},{32,16},{40,24},{48,32},{56,40},{64,48},{72,56},{80,... | collective-permute-start | bytes 147464 | tf_op jit(solution)/shard_map/ppermute | solution.py:23
  68.6 41.9 %collective-permute-start.8 = (f32[64,192]{1,0:T(8,128)S(1)}, f32[64,192]{1,0:T(8,128)S(1)}, u32[]{:S(2)}, u32[]{:S(2)}) collective-permute-start(f32[64,192]{1,0:T(8,128)S(1)} %get-tuple-element.34), channel_id=1, source_target_pairs={{248,0},{0,8},{8,16},{16,24},{24,32},{32,40},{40,48},{48,56},{56,6... | collective-permute-start | bytes 147464 | tf_op jit(solution)/shard_map/ppermute | solution.py:23
  68.7 39.0 %collective-permute-start.15 = (f32[64,192]{1,0:T(8,128)S(1)}, f32[64,192]{1,0:T(8,128)S(1)}, u32[]{:S(2)}, u32[]{:S(2)}) collective-permute-start(f32[64,192]{1,0:T(8,128)S(1)} %get-tuple-element.35), channel_id=1, source_target_pairs={{32,0},{40,8},{48,16},{56,24},{64,32},{72,40},{80,48},{88,56},{96,... | collective-permute-start | bytes 147464 | tf_op jit(solution)/shard_map/ppermute | solution.py:23
  68.8 35.2 %collective-permute-start.14 = (f32[64,192]{1,0:T(8,128)S(1)}, f32[64,192]{1,0:T(8,128)}, u32[]{:S(2)}, u32[]{:S(2)}) collective-permute-start(f32[64,192]{1,0:T(8,128)S(1)} %get-tuple-element.36), channel_id=1, source_target_pairs={{224,0},{232,8},{240,16},{248,24},{0,32},{8,40},{16,48},{24,56},{3... | collective-permute-start | bytes 147464 | tf_op jit(solution)/shard_map/ppermute | solution.py:23
  71.9 28.5 %collective-permute-start.13 = (f32[64,192]{1,0:T(8,128)S(1)}, f32[64,192]{1,0:T(8,128)}, u32[]{:S(2)}, u32[]{:S(2)}) collective-permute-start(f32[64,192]{1,0:T(8,128)S(1)} %get-tuple-element.37), channel_id=1, source_target_pairs={{24,0},{32,8},{40,16},{48,24},{56,32},{64,40},{72,48},{80,56},{88,... | collective-permute-start | bytes 147464 | tf_op jit(solution)/shard_map/ppermute | solution.py:23
  73.5 23.3 %collective-permute-start.12 = (f32[64,192]{1,0:T(8,128)S(1)}, f32[64,192]{1,0:T(8,128)}, u32[]{:S(2)}, u32[]{:S(2)}) collective-permute-start(f32[64,192]{1,0:T(8,128)S(1)} %get-tuple-element.38), channel_id=1, source_target_pairs={{232,0},{240,8},{248,16},{0,24},{8,32},{16,40},{24,48},{32,56},{40... | collective-permute-start | bytes 147464 | tf_op jit(solution)/shard_map/ppermute | solution.py:23
  76.5 42.9 %all-to-all-start.1 = ((s32[8,48,1]{1,2,0:T(1,128)}), s32[8,48,1]{1,2,0:T(1,128)}, u32[]{:S(2)}, u32[]{:S(2)}) async-start(s32[8,48,1]{1,2,0:T(1,128)} %bitcast.177), calls=%async_computation.1 | async-start | bytes 8192 | tf_op jit(solution)/shard_map/all_to_all | solution.py:84
  119.4 9.9 %all-to-all-start = ((f32[8,1,3072]{2,1,0:T(1,128)}), f32[8,1,3072]{2,1,0:T(1,128)}, u32[]{:S(2)}, u32[]{:S(2)}) async-start(f32[8,1,3072]{2,1,0:T(1,128)} %reshape.680), calls=%async_computation | async-start | bytes 196608 | tf_op jit(solution)/shard_map/all_to_all | solution.py:113
  124.2 150.4 %all-reduce.4.cloned.1.call-start = ((), (), s32[]{:S(2)}) async-start(), calls=%async_computation.5 | async-start | bytes 524288 | tf_op jit(solution)/shard_map/psum | solution.py:117
  136.3 603.0 %all-reduce.6.cloned.1.call-start = ((), (), s32[]{:S(2)}) async-start(), calls=%async_computation.6 | async-start | bytes 524288 | tf_op jit(solution)/shard_map/psum | solution.py:117
  364.0 11.2 %collective-permute-start.19 = (f32[64,192]{1,0:T(8,128)S(1)}, f32[64,192]{1,0:T(8,128)}, u32[]{:S(2)}, u32[]{:S(2)}) collective-permute-start(f32[64,192]{1,0:T(8,128)S(1)} %get-tuple-element.31), channel_id=1, source_target_pairs={{16,0},{24,8},{32,16},{40,24},{48,32},{56,40},{64,48},{72,56},{80,... | collective-permute-start | bytes 147464 | tf_op jit(solution)/shard_map/ppermute | solution.py:23
  366.0 9.2 collective-permute-start.18
  367.0 10.9 %collective-permute-start.17 = (f32[64,192]{1,0:T(8,128)S(1)}, f32[64,192]{1,0:T(8,128)}, u32[]{:S(2)}, u32[]{:S(2)}) collective-permute-start(f32[64,192]{1,0:T(8,128)S(1)} %get-tuple-element.33), channel_id=1, source_target_pairs={{8,0},{16,8},{24,16},{32,24},{40,32},{48,40},{56,48},{64,56},{72,6... | collective-permute-start | bytes 147464 | tf_op jit(solution)/shard_map/ppermute | solution.py:23
  371.5 20.5 %collective-permute-start.20 = (f32[64,192]{1,0:T(8,128)}, f32[64,192]{1,0:T(8,128)}, u32[]{:S(2)}, u32[]{:S(2)}) collective-permute-start(f32[64,192]{1,0:T(8,128)} %get-tuple-element.30), channel_id=1, source_target_pairs={{232,0},{240,8},{248,16},{0,24},{8,32},{16,40},{24,48},{32,56},{40... | collective-permute-start | bytes 147464 | tf_op jit(solution)/shard_map/ppermute | solution.py:23
  371.7 22.1 %collective-permute-start.21 = (f32[64,192]{1,0:T(8,128)}, f32[64,192]{1,0:T(8,128)}, u32[]{:S(2)}, u32[]{:S(2)}) collective-permute-start(f32[64,192]{1,0:T(8,128)} %get-tuple-element.29), channel_id=1, source_target_pairs={{24,0},{32,8},{40,16},{48,24},{56,32},{64,40},{72,48},{80,56},{88,... | collective-permute-start | bytes 147464 | tf_op jit(solution)/shard_map/ppermute | solution.py:23
  375.2 20.4 %collective-permute-start.22 = (f32[64,192]{1,0:T(8,128)}, f32[64,192]{1,0:T(8,128)}, u32[]{:S(2)}, u32[]{:S(2)}) collective-permute-start(f32[64,192]{1,0:T(8,128)} %get-tuple-element.28), channel_id=1, source_target_pairs={{224,0},{232,8},{240,16},{248,24},{0,32},{8,40},{16,48},{24,56},{3... | collective-permute-start | bytes 147464 | tf_op jit(solution)/shard_map/ppermute | solution.py:23
  375.2 22.2 %collective-permute-start.23 = (f32[64,192]{1,0:T(8,128)}, f32[64,192]{1,0:T(8,128)}, u32[]{:S(2)}, u32[]{:S(2)}) collective-permute-start(f32[64,192]{1,0:T(8,128)} %get-tuple-element.27), channel_id=1, source_target_pairs={{32,0},{40,8},{48,16},{56,24},{64,32},{72,40},{80,48},{88,56},{96,... | collective-permute-start | bytes 147464 | tf_op jit(solution)/shard_map/ppermute | solution.py:23
  377.9 21.3 %collective-permute-start.16 = (f32[64,192]{1,0:T(8,128)}, f32[64,192]{1,0:T(8,128)}, u32[]{:S(2)}, u32[]{:S(2)}) collective-permute-start(f32[64,192]{1,0:T(8,128)} %get-tuple-element.26), channel_id=1, source_target_pairs={{248,0},{0,8},{8,16},{16,24},{24,32},{32,40},{40,48},{48,56},{56,6... | collective-permute-start | bytes 147464 | tf_op jit(solution)/shard_map/ppermute | solution.py:23
  489.4 9.1 collective-permute-start.27
  492.3 8.8 collective-permute-start.25
  494.9 8.7 collective-permute-start.29
  498.5 8.8 collective-permute-start.31
  812.0 11.0 %collective-permute-start.35 = (f32[64,192]{1,0:T(8,128)S(1)}, f32[64,192]{1,0:T(8,128)S(1)}, u32[]{:S(2)}, u32[]{:S(2)}) collective-permute-start(f32[64,192]{1,0:T(8,128)S(1)} %get-tuple-element.15), channel_id=1, source_target_pairs={{16,0},{24,8},{32,16},{40,24},{48,32},{56,40},{64,48},{72,56},{80,... | collective-permute-start | bytes 147464 | tf_op jit(solution)/shard_map/ppermute | solution.py:23
  813.9 9.1 collective-permute-start.34
  814.9 10.8 %collective-permute-start.33 = (f32[64,192]{1,0:T(8,128)S(1)}, f32[64,192]{1,0:T(8,128)S(1)}, u32[]{:S(2)}, u32[]{:S(2)}) collective-permute-start(f32[64,192]{1,0:T(8,128)S(1)} %get-tuple-element.17), channel_id=1, source_target_pairs={{8,0},{16,8},{24,16},{32,24},{40,32},{48,40},{56,48},{64,56},{72,6... | collective-permute-start | bytes 147464 | tf_op jit(solution)/shard_map/ppermute | solution.py:23
  819.4 10.3 %collective-permute-start.37 = (f32[64,192]{1,0:T(8,128)}, f32[64,192]{1,0:T(8,128)}, u32[]{:S(2)}, u32[]{:S(2)}) collective-permute-start(f32[64,192]{1,0:T(8,128)} %get-tuple-element.13), channel_id=1, source_target_pairs={{24,0},{32,8},{40,16},{48,24},{56,32},{64,40},{72,48},{80,56},{88,... | collective-permute-start | bytes 147464 | tf_op jit(solution)/shard_map/ppermute | solution.py:23
  823.0 10.3 %collective-permute-start.39 = (f32[64,192]{1,0:T(8,128)S(1)}, f32[64,192]{1,0:T(8,128)}, u32[]{:S(2)}, u32[]{:S(2)}) collective-permute-start(f32[64,192]{1,0:T(8,128)S(1)} %get-tuple-element.11), channel_id=1, source_target_pairs={{32,0},{40,8},{48,16},{56,24},{64,32},{72,40},{80,48},{88,56},{96,... | collective-permute-start | bytes 147464 | tf_op jit(solution)/shard_map/ppermute | solution.py:23
  825.7 9.5 %collective-permute-start.32 = (f32[64,192]{1,0:T(8,128)S(1)}, f32[64,192]{1,0:T(8,128)}, u32[]{:S(2)}, u32[]{:S(2)}) collective-permute-start(f32[64,192]{1,0:T(8,128)S(1)} %get-tuple-element.10), channel_id=1, source_target_pairs={{248,0},{0,8},{8,16},{16,24},{24,32},{32,40},{40,48},{48,56},{56,6... | collective-permute-start | bytes 147464 | tf_op jit(solution)/shard_map/ppermute | solution.py:23
  (68 other events, 2427.3 us)
Sparse Core Ops, SparseCore 0:
  136.4 138.1 all-reduce.3
  603.2 136.1 all-reduce.5
